TPU v7x, 32 devices: a whole 2x2x4 slice. The times are simulated.
32 devices in a mesh: energy: 8 (over y, x, core), space: 4 (over z).
Axes of the slice: x: 2, y: 2, z: 4, core: 2. Of those that a mesh axis runs over, the one named last changes fastest.
Arguments:
- green: bfloat16 [4, 8, 4, 384, 384], P(None, 'energy', 'space'), may hold values from -6 to 6
- v_diag: bfloat16 [4, 384, 384], P('space'), may hold values from -0.3125 to 0.3125
- v_low: bfloat16 [4, 384, 384], P('space'), may hold values from -0.3125 to 0.3125
- energy_slot: int32 [8], replicated, may hold values from 0 to 7, each once
Outputs:
- sigma: bfloat16 [2, 8, 4, 384, 384], P(None, None, 'space', 'energy')
Inputs may be any that keep to these rules, and one draw needn't show every extreme that they name: `energy_slot`: each grid energy appears in exactly one slot.
All inputs are finite; a program needn't handle non-finite values.
Results may differ from a plain program's by a relative error of at most 0.0066.
Values may be sent and summed in bfloat16 or wider, within the bound.
No kernel may reach another device: no remote copies, remote signals or barrier semaphores. Data moves between devices by JAX's collectives and lax.ppermute only.
A program may use at most 64 MiB of HBM per device.

v0:
```python
import math
import jax
import jax.numpy as jnp
from jax import lax
from jax.sharding import PartitionSpec as P


def shifted(value, axis, steps):
    count = lax.axis_size(axis)
    leading, last = (max(0, -steps), min(count, count - steps))
    return lax.ppermute(value, axis, [(source, source + steps) for source in range(leading, last)])


def apply_table(table, values):
    return jnp.dot(
        table, values, precision=lax.Precision.HIGHEST, preferred_element_type=jnp.float32
    )


def spectra(cos_table, sin_table, real_part, imag_part):
    out_real = apply_table(cos_table, real_part) + apply_table(sin_table, imag_part)
    out_imag = apply_table(cos_table, imag_part) - apply_table(sin_table, real_part)
    return (out_real, out_imag)


def to_slots(cos_table, sin_table, real_part, imag_part):
    factor = 1.0 / cos_table.shape[0]
    cos_back = cos_table.T
    sin_back = sin_table.T
    out_real = (apply_table(cos_back, real_part) - apply_table(sin_back, imag_part)) * factor
    out_imag = (apply_table(cos_back, imag_part) + apply_table(sin_back, real_part)) * factor
    return (out_real, out_imag)


def sandwich(matrix, polar):
    left = jnp.einsum("ij,cejk->ceik", matrix, polar, preferred_element_type=jnp.float32).astype(
        jnp.bfloat16
    )
    return jnp.einsum("ceij,kj->ceik", left, matrix, preferred_element_type=jnp.float32)


def sandwich_t(matrix, polar):
    left = jnp.einsum("ji,cejk->ceik", matrix, polar, preferred_element_type=jnp.float32).astype(
        jnp.bfloat16
    )
    return jnp.einsum("ceij,jk->ceik", left, matrix, preferred_element_type=jnp.float32)


def shards(green, v_diag, v_low, energy_slot):
    energies = energy_slot.shape[0]
    period = 2 * energies
    frequency = jnp.arange(period, dtype=jnp.int32)
    phases = frequency[:, None] * energy_slot[None, :] % period
    angles = phases.astype(jnp.float32) * (2.0 * math.pi / period)
    cos_table = jnp.cos(angles)
    sin_table = jnp.sin(angles)
    scaling = energies ** (-0.5)
    arrived = lax.all_to_all(green[:, :, 0], "energy", split_axis=2, concat_axis=1, tiled=True)
    row_count = arrived.shape[2]
    col_count = arrived.shape[3]
    flattened = arrived.reshape((4, energies, row_count * col_count)).astype(jnp.float32)
    lesser_re, lesser_im = spectra(cos_table, sin_table, flattened[0], flattened[1])
    greater_re, greater_im = spectra(cos_table, sin_table, flattened[2], flattened[3])
    cross_re = lesser_re * greater_re + lesser_im * greater_im
    cross_im = lesser_im * greater_re - lesser_re * greater_im
    corr_re, corr_im = to_slots(cos_table, sin_table, cross_re, cross_im)
    polar_slot = (
        jnp.stack([corr_im * scaling, -corr_re * scaling])
        .reshape((2, energies, row_count, col_count))
        .astype(jnp.bfloat16)
    )
    polar = lax.all_to_all(polar_slot, "energy", split_axis=1, concat_axis=2, tiled=True)
    diagonal = v_diag[0]
    lower = v_low[0]
    own_term = sandwich(diagonal, polar)
    below = shifted(polar, "space", 1)
    handed = sandwich_t(lower, polar).astype(jnp.bfloat16)
    received = shifted(handed, "space", -1)
    total = own_term + sandwich(lower, below) + received.astype(jnp.float32)
    screened = total.astype(jnp.bfloat16)
    screened_rows = lax.all_to_all(screened, "energy", split_axis=2, concat_axis=1, tiled=True)
    weights = screened_rows.reshape((2, energies, row_count * col_count)).astype(jnp.float32)
    weight_re, weight_im = spectra(cos_table, sin_table, weights[0], weights[1])
    joint_re = lesser_re * weight_re - lesser_im * weight_im
    joint_im = lesser_re * weight_im + lesser_im * weight_re
    conv_re, conv_im = to_slots(cos_table, sin_table, joint_re, joint_im)
    sigma = (
        jnp.stack([-conv_im * scaling, conv_re * scaling])
        .reshape((2, energies, row_count, col_count))
        .astype(jnp.bfloat16)
    )
    return sigma[:, :, None]


def solution(mesh):
    in_specs = (
        P(None, "energy", "space", None, None),
        P("space", None, None),
        P("space", None, None),
        P(),
    )
    out_specs = P(None, None, "space", "energy", None)
    return jax.shard_map(shards, mesh=mesh, in_specs=in_specs, out_specs=out_specs, check_vma=False)
```

profile of v0, /device:TPU:24, one launch (start us, length us, event | category | flops | bytes accessed | tf_op | source)
XLA Modules:
  0.0 103.2 jit_solution(476986298993754648)
XLA Ops:
  0.0 2.2 %copy.56 = bf16[4,1,1,384,384]{4,0,3,2,1:T(4,128)(2,1)S(1)} copy(bf16[4,1,1,384,384]{4,3,2,1,0:T(8,128)(2,1)} %param.4) | data formatting | bytes 2359296 | tf_op args[0]
  2.2 20.3 %all_to_all.30 = bf16[4,1,384,384]{3,0,1,2:T(4,128)(2,1)S(1)} all-to-all(bf16[4,1,384,384]{3,0,1,2:T(4,128)(2,1)S(1)} %bitcast.85), channel_id=1, replica_groups=mesh['energy'=8,'space'=4] {'energy'}, dimensions={2} | all-to-all | bytes 2359296 | tf_op jit(solution)/shard_map/all_to_all | solution.py:58
  22.5 7.5 %slice_reduce_fusion.3 = (bf16[384,384]{1,0:T(8,128)(2,1)S(1)}, bf16[384,384]{1,0:T(8,128)(2,1)S(1)}, bf16[384,384]{1,0:T(8,128)(2,1)S(1)}, bf16[384,384]{1,0:T(8,128)(2,1)S(1)}) fusion(bf16[4,1,384,384]{3,0,1,2:T(4,128)(2,1)S(1)} %all_to_all.30), kind=kLoop, calls=%fused_computation.42 | loop fusion | bytes 2359296 | tf_op jit(solution)/shard_map/slice | solution.py:63
  30.0 0.0 copy-start.3
  30.0 0.1 squeeze.30
  30.2 0.1 squeeze.31
  30.3 0.1 squeeze.29
  30.5 0.1 squeeze.28
  30.6 0.1 copy-done.3
  30.7 0.7 fusion.52
  31.4 0.7 fusion.50
  32.0 0.7 convolution_subtract_fusion.2
  32.7 0.7 fusion.46
  33.4 0.7 fusion.48
  34.0 0.7 convolution_subtract_fusion.1
  34.7 0.7 convolution_add_fusion.1
  35.4 2.1 %multiply_subtract_fusion.1 = (f32[16,18432]{1,0:T(8,128)S(1)}, f32[16,18432]{1,0:T(8,128)S(1)}, f32[16,18432]{1,0:T(8,128)}) fusion(f32[16,18432]{1,0:T(8,128)S(1)} %convolution_subtract_fusion.1, f32[16,18432]{1,0:T(8,128)S(1)} %convolution_subtract_fusion.2, f32[16,18432]{1,0:T(8,128)S(1)} %convolution_add_fusion.1, f32[16,18432]{1,0:T(8,128)S(1)} %fusion.52, ...), kind=kOutput, calls=%fused_computation.38 | convolution fusion | flops 30377728 | bytes 8552480 | tf_op jit(solution)/shard_map/dot_general | solution.py:15
  37.4 0.7 fusion.44
  38.2 0.7 fusion.42
  38.9 0.8 fusion.8
  39.7 0.8 fusion.9
  40.5 0.1 pad_maximum_fusion
  40.6 12.8 %all_to_all.31 = bf16[2,8,48,384]{3,2,0,1:T(8,128)(2,1)S(1)} all-to-all(bf16[2,8,48,384]{3,2,0,1:T(8,128)(2,1)S(1)} %pad_maximum_fusion), channel_id=1, replica_groups=mesh['energy'=8,'space'=4] {'energy'}, dimensions={1} | all-to-all | bytes 1179648 | tf_op jit(solution)/shard_map/all_to_all | solution.py:72
  53.4 0.1 copy.39
  53.5 1.1 %copy.43 = bf16[2,1,384,384]{2,3,0,1:T(8,128)(2,1)} copy(bf16[2,1,384,384]{3,2,0,1:T(8,128)(2,1)S(1)} %bitcast.82) | data formatting | bytes 1179648 | tf_op jit(solution)/shard_map/all_to_all | solution.py:72
  54.6 1.9 %fusion.17 = bf16[2,1,384,384]{3,2,0,1:T(8,128)(2,1)} fusion(bf16[2,384,384]{2,1,0:T(8,128)(2,1)S(1)} %bitcast.83, bf16[1,384,384]{2,1,0:T(8,128)(2,1)S(1)} %copy-done), kind=kOutput, calls=%fused_computation.32 | convolution fusion | flops 453574656 | bytes 1474560 | tf_op jit(solution)/shard_map/ceij,jk->ceik/dot_general | solution.py:46
  56.5 3.2 %collective-permute-start.1 = (bf16[2,1,384,384]{3,2,0,1:T(8,128)(2,1)}, bf16[2,1,384,384]{3,2,0,1:T(8,128)(2,1)}, u32[]{:S(2)}, u32[]{:S(2)}) collective-permute-start(bf16[2,1,384,384]{3,2,0,1:T(8,128)(2,1)} %fusion.17), channel_id=1, source_target_pairs={{1,0},{2,1},{3,2},{5,4},{6,5},{7,6},{9,8},{10,9},{11,10},{13,12},{... | collective-permute-start | bytes 1769480 | tf_op jit(solution)/shard_map/ppermute | solution.py:11
  59.7 1.5 %collective-permute-start = (bf16[2,1,384,384]{2,3,0,1:T(8,128)(2,1)}, bf16[2,1,384,384]{2,3,0,1:T(8,128)(2,1)}, u32[]{:S(2)}, u32[]{:S(2)}) collective-permute-start(bf16[2,1,384,384]{2,3,0,1:T(8,128)(2,1)} %copy.43), channel_id=1, source_target_pairs={{0,1},{1,2},{2,3},{4,5},{5,6},{6,7},{8,9},{9,10},{10,11},{12,13},{... | collective-permute-start | bytes 1769480 | tf_op jit(solution)/shard_map/ppermute | solution.py:11
  61.2 0.0 copy-done.2
  61.2 1.1 %fusion.14 = f32[2,384,384]{2,1,0:T(8,128)S(1)} fusion(bf16[2,384,384]{2,1,0:T(8,128)(2,1)S(1)} %bitcast.84, bf16[1,384,384]{2,1,0:T(8,128)(2,1)S(1)} %copy-done.2), kind=kOutput, calls=%fused_computation.29 | convolution fusion | flops 453279744 | bytes 2064384 | tf_op jit(solution)/shard_map/ceij,kj->ceik/dot_general | solution.py:39
  62.3 9.4 %collective-permute-done.1 = bf16[2,1,384,384]{3,2,0,1:T(8,128)(2,1)} collective-permute-done((bf16[2,1,384,384]{3,2,0,1:T(8,128)(2,1)}, bf16[2,1,384,384]{3,2,0,1:T(8,128)(2,1)}, u32[]{:S(2)}, u32[]{:S(2)}) %collective-permute-start.1) | collective-permute-done | bytes 589856 | tf_op jit(solution)/shard_map/ppermute | solution.py:11
  71.6 5.0 %collective-permute-done = bf16[2,1,384,384]{2,3,0,1:T(8,128)(2,1)} collective-permute-done((bf16[2,1,384,384]{2,3,0,1:T(8,128)(2,1)}, bf16[2,1,384,384]{2,3,0,1:T(8,128)(2,1)}, u32[]{:S(2)}, u32[]{:S(2)}) %collective-permute-start) | collective-permute-done | bytes 589856 | tf_op jit(solution)/shard_map/ppermute | solution.py:11
  76.6 2.3 %add_convert_fusion = bf16[2,1,384,384]{3,2,0,1:T(8,128)(2,1)S(1)} fusion(bf16[2,1,384,384]{3,2,0,1:T(8,128)(2,1)} %collective-permute-done.1, f32[2,384,384]{2,1,0:T(8,128)S(1)} %fusion.14, bf16[2,1,384,384]{2,3,0,1:T(8,128)(2,1)} %collective-permute-done, bf16[1,384,384]{2,1,0:T(8,128)(2,1)S(1)} %copy-done), kind=kOutput, calls=%fused_computation.36 | convolution fusion | flops 454459392 | bytes 3244032 | tf_op jit(solution)/shard_map/ceij,kj->ceik/dot_general | solution.py:39
  78.9 0.6 copy.47
  79.5 12.8 %all_to_all.32 = bf16[2,1,384,384]{3,0,1,2:T(2,128)(2,1)S(1)} all-to-all(bf16[2,1,384,384]{3,0,1,2:T(2,128)(2,1)S(1)} %copy.47), channel_id=1, replica_groups=mesh['energy'=8,'space'=4] {'energy'}, dimensions={2} | all-to-all | bytes 1179648 | tf_op jit(solution)/shard_map/all_to_all | solution.py:81
  92.3 2.9 %slice_reduce_fusion = (bf16[384,384]{1,0:T(8,128)(2,1)S(1)}, bf16[384,384]{1,0:T(8,128)(2,1)S(1)}) fusion(bf16[2,1,384,384]{3,0,1,2:T(2,128)(2,1)S(1)} %all_to_all.32), kind=kLoop, calls=%fused_computation.39 | loop fusion | bytes 1179648 | tf_op jit(solution)/shard_map/slice | solution.py:83
  95.2 0.1 squeeze.35
  95.4 0.1 squeeze.34
  95.5 0.7 fusion.40
  96.2 0.7 fusion.38
  96.9 0.7 convolution_subtract_fusion
  97.6 0.6 copy-done.1
  98.1 1.0 %multiply_add_fusion = (f32[16,18432]{1,0:T(8,128)S(1)}, f32[16,18432]{1,0:T(8,128)S(1)}) fusion(f32[16,18432]{1,0:T(8,128)S(1)} %convolution_subtract_fusion.2, f32[16,18432]{1,0:T(8,128)S(1)} %copy-done.1, f32[16,18432]{1,0:T(8,128)S(1)} %convolution_subtract_fusion, f32[16,18432]{1,0:T(8,128)S(1)} %fusion.38, bf16[8,18432]{1,0:T(8,128)(2,1)S(1)} %squeeze.34, ...), kind=kOutput, calls=%fused_computation.35 | convolution fusion | flops 30377728 | bytes 7372832 | tf_op jit(solution)/shard_map/dot_general | solution.py:15
  99.2 0.7 fusion.36
  99.9 0.7 fusion.34
  100.7 0.8 fusion.10
  101.5 0.7 fusion.11
  102.3 0.9 pad_maximum_fusion.1
  (8 shorter events, 0.2 us)
Async XLA Ops:
  0.0 54.6 %copy-start = (bf16[1,384,384]{2,1,0:T(8,128)(2,1)S(1)}, bf16[1,384,384]{2,1,0:T(8,128)(2,1)}, u32[]{:S(2)}) copy-start(bf16[1,384,384]{2,1,0:T(8,128)(2,1)} %param.6) | copy-start | bytes 884740
  30.0 0.7 copy-start.3
  54.6 6.6 %copy-start.2 = (bf16[1,384,384]{2,1,0:T(8,128)(2,1)S(1)}, bf16[1,384,384]{2,1,0:T(8,128)(2,1)}, u32[]{:S(2)}) copy-start(bf16[1,384,384]{2,1,0:T(8,128)(2,1)} %param.5) | copy-start | bytes 884740
  56.5 15.2 %collective-permute-start.1 = (bf16[2,1,384,384]{3,2,0,1:T(8,128)(2,1)}, bf16[2,1,384,384]{3,2,0,1:T(8,128)(2,1)}, u32[]{:S(2)}, u32[]{:S(2)}) collective-permute-start(bf16[2,1,384,384]{3,2,0,1:T(8,128)(2,1)} %fusion.17), channel_id=1, source_target_pairs={{1,0},{2,1},{3,2},{5,4},{6,5},{7,6},{9,8},{10,9},{11,10},{13,12},{... | collective-permute-start | bytes 1769480 | tf_op jit(solution)/shard_map/ppermute | solution.py:11
  59.7 16.9 %collective-permute-start = (bf16[2,1,384,384]{2,3,0,1:T(8,128)(2,1)}, bf16[2,1,384,384]{2,3,0,1:T(8,128)(2,1)}, u32[]{:S(2)}, u32[]{:S(2)}) collective-permute-start(bf16[2,1,384,384]{2,3,0,1:T(8,128)(2,1)} %copy.43), channel_id=1, source_target_pairs={{0,1},{1,2},{2,3},{4,5},{5,6},{6,7},{8,9},{9,10},{10,11},{12,13},{... | collective-permute-start | bytes 1769480 | tf_op jit(solution)/shard_map/ppermute | solution.py:11
  96.9 1.3 %copy-start.1 = (f32[16,18432]{1,0:T(8,128)S(1)}, f32[16,18432]{1,0:T(8,128)}, u32[]{:S(2)}) copy-start(f32[16,18432]{1,0:T(8,128)} %get-tuple-element.15) | copy-start | bytes 3538948
where the time goes:
time: 104 us; the launch traced here: 103 us
  blocking collectives  45.9 us (44%)
  matrix products  20.9 us (20%)
  local copies, waits for them, and re-layouts  16.1 us (15%)
  waiting for transfers between devices  14.3 us (14%)
  starting transfers between devices  4.7 us (5%)
    all_to_all x1, blocking collectives, shards(): lax.all_to_all(green[:, :, 0], 'energy', split_axis=2, concat_axis=1, til...  20.3 us
    dot_general x20, matrix products, apply_table(): jnp.dot(table, values, precision=lax.Precision.HIGHEST, preferred_element...  15.7 us
    ppermute x2, waiting for transfers between devices, shifted(): lax.ppermute(value, axis, [(source, source + steps) for source in range(l...  14.3 us
    all_to_all x1, blocking collectives, shards(): lax.all_to_all(polar_slot, 'energy', split_axis=1, concat_axis=2, tiled=T...  12.8 us
    all_to_all x1, blocking collectives, shards(): lax.all_to_all(screened, 'energy', split_axis=2, concat_axis=1, tiled=True)  12.8 us
    slice x1, local copies, waits for them, and re-layouts, shards(): flattened[2]  7.53 us
    ppermute x2, starting transfers between devices, shifted(): lax.ppermute(value, axis, [(source, source + steps) for source in range(l...  4.7 us
    dot_general x2, matrix products, sandwich(): jnp.einsum('ceij,kj->ceik', left, matrix, preferred_element_type=jnp.floa...  3.35 us
  transfers between devices with their start and end apart: 2, of which 2 were waited for; matrix products, arithmetic and copies ran while one was open for 1% of the time, Pallas kernels for 0%

commit v1 on v0

--- a/solution.py
+++ b/solution.py
@@ -3,6 +3,28 @@
 import jax.numpy as jnp
 from jax import lax
 from jax.sharding import PartitionSpec as P
+
+
+def in_blocks(x, dim, size):
+    before, after = (x.shape[:dim], x.shape[dim + 1 :])
+    return jnp.moveaxis(x.reshape(*before, size, -1, *after), dim, 0)
+
+
+def laid_out(tiles, dim):
+    lengths = list(tiles.shape[1:])
+    lengths[dim] *= tiles.shape[0]
+    return jnp.moveaxis(tiles, 0, dim).reshape(lengths)
+
+
+def pairwise_exchange(shard, axis, split_dim, concat_dim):
+    length, index = (lax.axis_size(axis), lax.axis_index(axis))
+    blocks = in_blocks(shard, split_dim, length)
+    gathered = [blocks[index]]
+    for turn in range(1, length):
+        sent = blocks[index ^ turn]
+        gathered.append(lax.ppermute(sent, axis, [(i, i ^ turn) for i in range(length)]))
+    blocks = jnp.stack(gathered)[index ^ jnp.arange(length)]
+    return laid_out(blocks, concat_dim)
 
 
 def shifted(value, axis, steps):
@@ -55,7 +77,7 @@
     cos_table = jnp.cos(angles)
     sin_table = jnp.sin(angles)
     scaling = energies ** (-0.5)
-    arrived = lax.all_to_all(green[:, :, 0], "energy", split_axis=2, concat_axis=1, tiled=True)
+    arrived = pairwise_exchange(green[:, :, 0], "energy", 2, 1)
     row_count = arrived.shape[2]
     col_count = arrived.shape[3]
     flattened = arrived.reshape((4, energies, row_count * col_count)).astype(jnp.float32)

time: 104 us -> 95.6 us (0.919)
  blocking collectives: 45.9 us -> 25.8 us
  waiting for transfers between devices: 14.3 us -> 25.6 us
  starting transfers between devices: 4.7 us -> 11.8 us
  local copies, waits for them, and re-layouts: 16.1 us -> 9.77 us
    all_to_all x1 -> x0, blocking collectives: 20.3 us -> none  [shards(): lax.all_to_all(green[:, :, 0], 'energy', split_axis=2, concat_axis=1, til...]
    ppermute x0 -> x7, waiting for transfers between devices: none -> 11.3 us  [pairwise_exchange(): lax.ppermute(sent, axis, [(i, i ^ turn) for i in range(length)])]
    slice x1 -> x0, local copies, waits for them, and re-layouts: 7.53 us -> none  [shards(): flattened[2]]
    ppermute x0 -> x7, starting transfers between devices: none -> 7.14 us  [pairwise_exchange(): lax.ppermute(sent, axis, [(i, i ^ turn) for i in range(length)])]
    unnamed x9 -> x20, local copies, waits for them, and re-layouts: 2.88 us -> 2.42 us
  transfers between devices with their start and end apart: 2 -> 9, of which waited for: 2 -> 5; matrix products, arithmetic and copies ran while one was open for 1% -> 2% of each run, Pallas kernels for 0% -> 0%
where the time goes in v1:
time: 95.6 us; the launch traced here: 95.3 us
  blocking collectives  25.8 us (27%)
  waiting for transfers between devices  25.6 us (27%)
  matrix products  21 us (22%)
  starting transfers between devices  11.8 us (12%)
  local copies, waits for them, and re-layouts  9.77 us (10%)
  other arithmetic  0.97 us (1%)
    dot_general x20, matrix products, apply_table(): jnp.dot(table, values, precision=lax.Precision.HIGHEST, preferred_element...  15.7 us
    ppermute x2, waiting for transfers between devices, shifted(): lax.ppermute(value, axis, [(source, source + steps) for source in range(l...  14.4 us
    all_to_all x1, blocking collectives, shards(): lax.all_to_all(polar_slot, 'energy', split_axis=1, concat_axis=2, tiled=T...  13 us
    all_to_all x1, blocking collectives, shards(): lax.all_to_all(screened, 'energy', split_axis=2, concat_axis=1, tiled=True)  12.8 us
    ppermute x7, waiting for transfers between devices, pairwise_exchange(): lax.ppermute(sent, axis, [(i, i ^ turn) for i in range(length)])  11.3 us
    ppermute x7, starting transfers between devices, pairwise_exchange(): lax.ppermute(sent, axis, [(i, i ^ turn) for i in range(length)])  7.14 us
    ppermute x2, starting transfers between devices, shifted(): lax.ppermute(value, axis, [(source, source + steps) for source in range(l...  4.63 us
    dot_general x2, matrix products, sandwich(): jnp.einsum('ceij,kj->ceik', left, matrix, preferred_element_type=jnp.floa...  3.34 us
  transfers between devices with their start and end apart: 9, of which 5 were waited for; matrix products, arithmetic and copies ran while one was open for 2% of the time, Pallas kernels for 0%

profile of v1, /device:TPU:24, one launch (start us, length us, event | category | flops | bytes accessed | tf_op | source)
XLA Modules:
  0.0 95.3 jit_solution(13473231912697713155)
XLA Ops:
  0.0 1.4 %dynamic-slice_bitcast_fusion = (bf16[4,1,48,384]{3,2,0,1:T(8,128)(2,1)S(1)}, bf16[4,1,48,384]{3,2,0,1:T(8,128)(2,1)S(1)}, bf16[4,1,48,384]{3,2,0,1:T(8,128)(2,1...) fusion(bf16[4,1,8,48,384]{4,3,2,0,1:T(8,128)(2,1)} %bitcast.153, ...), kind=kLoop, calls=%fused_computation.59 | loop fusion | bytes 2064412 | tf_op jit(solution)/shard_map/squeeze | solution.py:24
  1.4 2.0 %collective-permute-start.6 = (bf16[4,1,48,384]{3,2,0,1:T(8,128)(2,1)S(1)}, bf16[4,1,48,384]{3,2,0,1:T(8,128)(2,1)S(1)}, u32[]{:S(2)}, u32[]{:S(2)}) collective-permute-start(bf16[4,1,48,384]{3,2,0,1:T(8,128)(2,1)S(1)} %get-tuple-element.15), channel_id=1, source_target_pairs={{0,28},{4,24},{8,20},{12,16},{16,12},{20,8},{24,4},{28,0},{1,29},{... | collective-permute-start | bytes 442376 | tf_op jit(solution)/shard_map/ppermute | solution.py:25
  3.4 0.6 collective-permute-start.5
  4.0 1.4 %collective-permute-start.4 = (bf16[4,1,48,384]{3,2,0,1:T(8,128)(2,1)S(1)}, bf16[4,1,48,384]{3,2,0,1:T(8,128)(2,1)S(1)}, u32[]{:S(2)}, u32[]{:S(2)}) collective-permute-start(bf16[4,1,48,384]{3,2,0,1:T(8,128)(2,1)S(1)} %get-tuple-element.17), channel_id=1, source_target_pairs={{0,20},{4,16},{8,28},{12,24},{16,4},{20,0},{24,12},{28,8},{1,21},{... | collective-permute-start | bytes 442376 | tf_op jit(solution)/shard_map/ppermute | solution.py:25
  5.4 0.5 collective-permute-start.3
  5.9 0.9 bitcast_dynamic-update-slice_fusion.7
  6.9 0.4 collective-permute-done
  7.3 1.5 %collective-permute-start.1 = (bf16[4,1,48,384]{3,2,0,1:T(8,128)(2,1)S(1)}, bf16[4,1,48,384]{3,2,0,1:T(8,128)(2,1)S(1)}, u32[]{:S(2)}, u32[]{:S(2)}) collective-permute-start(bf16[4,1,48,384]{3,2,0,1:T(8,128)(2,1)S(1)} %get-tuple-element.20), channel_id=1, source_target_pairs={{0,8},{4,12},{8,0},{12,4},{16,24},{20,28},{24,16},{28,20},{1,9},{5... | collective-permute-start | bytes 442376 | tf_op jit(solution)/shard_map/ppermute | solution.py:25
  8.8 6.2 %collective-permute-done.1 = bf16[4,1,48,384]{3,2,0,1:T(8,128)(2,1)S(1)} collective-permute-done((bf16[4,1,48,384]{3,2,0,1:T(8,128)(2,1)S(1)}, bf16[4,1,48,384]{3,2,0,1:T(8,128)(2,1)S(1)}, u32[]{:S(2)}, u32[]{:S(2)}) %collective-permute-start.1) | collective-permute-done | bytes 147488 | tf_op jit(solution)/shard_map/ppermute | solution.py:25
  15.0 1.2 %collective-permute-start.2 = (bf16[4,1,48,384]{3,2,0,1:T(8,128)(2,1)S(1)}, bf16[4,1,48,384]{3,2,0,1:T(8,128)(2,1)S(1)}, u32[]{:S(2)}, u32[]{:S(2)}) collective-permute-start(bf16[4,1,48,384]{3,2,0,1:T(8,128)(2,1)S(1)} %get-tuple-element.19), channel_id=1, source_target_pairs={{0,12},{4,8},{8,4},{12,0},{16,28},{20,24},{24,20},{28,16},{1,13},{... | collective-permute-start | bytes 442376 | tf_op jit(solution)/shard_map/ppermute | solution.py:25
  16.2 4.6 %collective-permute-done.2 = bf16[4,1,48,384]{3,2,0,1:T(8,128)(2,1)S(1)} collective-permute-done((bf16[4,1,48,384]{3,2,0,1:T(8,128)(2,1)S(1)}, bf16[4,1,48,384]{3,2,0,1:T(8,128)(2,1)S(1)}, u32[]{:S(2)}, u32[]{:S(2)}) %collective-permute-start.2) | collective-permute-done | bytes 147488 | tf_op jit(solution)/shard_map/ppermute | solution.py:25
  21.1 0.8 gather_fusion
  22.3 0.4 copy-done.3
  22.7 0.7 fusion.52
  23.3 0.7 fusion.50
  24.0 0.7 convolution_subtract_fusion.2
  24.7 0.7 fusion.46
  25.3 0.7 fusion.48
  26.0 0.7 convolution_subtract_fusion.1
  26.7 0.7 convolution_add_fusion.1
  27.3 2.1 %multiply_subtract_fusion.1 = (f32[16,18432]{1,0:T(8,128)S(1)}, f32[16,18432]{1,0:T(8,128)S(1)}, f32[16,18432]{1,0:T(8,128)}) fusion(f32[16,18432]{1,0:T(8,128)S(1)} %convolution_subtract_fusion.1, f32[16,18432]{1,0:T(8,128)S(1)} %convolution_subtract_fusion.2, f32[16,18432]{1,0:T(8,128)S(1)} %convolution_add_fusion.1, f32[16,18432]{1,0:T(8,128)S(1)} %fusion.52, ...), kind=kOutput, calls=%fused_computation.38 | convolution fusion | flops 30377728 | bytes 8552480 | tf_op jit(solution)/shard_map/dot_general | solution.py:37
  29.4 0.7 fusion.44
  30.2 0.7 fusion.42
  30.9 0.7 fusion.8
  31.7 0.8 fusion.9
  32.6 13.0 %all_to_all.21 = bf16[2,8,48,384]{3,2,0,1:T(8,128)(2,1)S(1)} all-to-all(bf16[2,8,48,384]{3,2,0,1:T(8,128)(2,1)S(1)} %pad_maximum_fusion), channel_id=1, replica_groups=mesh['energy'=8,'space'=4] {'energy'}, dimensions={1} | all-to-all | bytes 1179648 | tf_op jit(solution)/shard_map/all_to_all | solution.py:94
  45.7 1.1 %copy.41 = bf16[2,1,384,384]{2,3,0,1:T(8,128)(2,1)} copy(bf16[2,1,384,384]{3,2,0,1:T(8,128)(2,1)S(1)} %bitcast.136) | data formatting | bytes 1179648 | tf_op jit(solution)/shard_map/all_to_all | solution.py:94
  46.7 1.9 %fusion.17 = bf16[2,1,384,384]{3,2,0,1:T(8,128)(2,1)} fusion(bf16[2,384,384]{2,1,0:T(8,128)(2,1)S(1)} %bitcast.137, bf16[1,384,384]{2,1,0:T(8,128)(2,1)S(1)} %copy-done), kind=kOutput, calls=%fused_computation.33 | convolution fusion | flops 453574656 | bytes 1474560 | tf_op jit(solution)/shard_map/ceij,jk->ceik/dot_general | solution.py:68
  48.6 3.2 %collective-permute-start.8 = (bf16[2,1,384,384]{3,2,0,1:T(8,128)(2,1)}, bf16[2,1,384,384]{3,2,0,1:T(8,128)(2,1)}, u32[]{:S(2)}, u32[]{:S(2)}) collective-permute-start(bf16[2,1,384,384]{3,2,0,1:T(8,128)(2,1)} %fusion.17), channel_id=1, source_target_pairs={{1,0},{2,1},{3,2},{5,4},{6,5},{7,6},{9,8},{10,9},{11,10},{13,12},{... | collective-permute-start | bytes 1769480 | tf_op jit(solution)/shard_map/ppermute | solution.py:33
  51.8 1.5 %collective-permute-start.7 = (bf16[2,1,384,384]{2,3,0,1:T(8,128)(2,1)}, bf16[2,1,384,384]{2,3,0,1:T(8,128)(2,1)}, u32[]{:S(2)}, u32[]{:S(2)}) collective-permute-start(bf16[2,1,384,384]{2,3,0,1:T(8,128)(2,1)} %copy.41), channel_id=1, source_target_pairs={{0,1},{1,2},{2,3},{4,5},{5,6},{6,7},{8,9},{9,10},{10,11},{12,13},{... | collective-permute-start | bytes 1769480 | tf_op jit(solution)/shard_map/ppermute | solution.py:33
  53.3 1.1 %fusion.14 = f32[2,384,384]{2,1,0:T(8,128)S(1)} fusion(bf16[2,384,384]{2,1,0:T(8,128)(2,1)S(1)} %bitcast.138, bf16[1,384,384]{2,1,0:T(8,128)(2,1)S(1)} %copy-done.2), kind=kOutput, calls=%fused_computation.30 | convolution fusion | flops 453279744 | bytes 2064384 | tf_op jit(solution)/shard_map/ceij,kj->ceik/dot_general | solution.py:61
  54.3 9.4 %collective-permute-done.8 = bf16[2,1,384,384]{3,2,0,1:T(8,128)(2,1)} collective-permute-done((bf16[2,1,384,384]{3,2,0,1:T(8,128)(2,1)}, bf16[2,1,384,384]{3,2,0,1:T(8,128)(2,1)}, u32[]{:S(2)}, u32[]{:S(2)}) %collective-permute-start.8) | collective-permute-done | bytes 589856 | tf_op jit(solution)/shard_map/ppermute | solution.py:33
  63.8 4.9 %collective-permute-done.7 = bf16[2,1,384,384]{2,3,0,1:T(8,128)(2,1)} collective-permute-done((bf16[2,1,384,384]{2,3,0,1:T(8,128)(2,1)}, bf16[2,1,384,384]{2,3,0,1:T(8,128)(2,1)}, u32[]{:S(2)}, u32[]{:S(2)}) %collective-permute-start.7) | collective-permute-done | bytes 589856 | tf_op jit(solution)/shard_map/ppermute | solution.py:33
  68.7 2.3 %add_convert_fusion = bf16[2,1,384,384]{3,2,0,1:T(8,128)(2,1)S(1)} fusion(bf16[2,1,384,384]{3,2,0,1:T(8,128)(2,1)} %collective-permute-done.8, f32[2,384,384]{2,1,0:T(8,128)S(1)} %fusion.14, bf16[2,1,384,384]{2,3,0,1:T(8,128)(2,1)} %collective-permute-done.7, bf16[1,384,384]{2,1,0:T(8,128)(2,1)S(1)} %copy-done), kind=kOutput, calls=%fused_computation.36 | convolution fusion | flops 454459392 | bytes 3244032 | tf_op jit(solution)/shard_map/ceij,kj->ceik/dot_general | solution.py:61
  71.0 0.6 copy.45
  71.6 12.8 %all_to_all.22 = bf16[2,1,384,384]{3,0,1,2:T(2,128)(2,1)S(1)} all-to-all(bf16[2,1,384,384]{3,0,1,2:T(2,128)(2,1)S(1)} %copy.45), channel_id=1, replica_groups=mesh['energy'=8,'space'=4] {'energy'}, dimensions={2} | all-to-all | bytes 1179648 | tf_op jit(solution)/shard_map/all_to_all | solution.py:103
  84.4 2.9 %slice_reduce_fusion = (bf16[384,384]{1,0:T(8,128)(2,1)S(1)}, bf16[384,384]{1,0:T(8,128)(2,1)S(1)}) fusion(bf16[2,1,384,384]{3,0,1,2:T(2,128)(2,1)S(1)} %all_to_all.22), kind=kLoop, calls=%fused_computation.39 | loop fusion | bytes 1179648 | tf_op jit(solution)/shard_map/slice | solution.py:105
  87.3 0.1 squeeze.59
  87.6 0.7 fusion.40
  88.3 0.7 fusion.38
  89.0 0.7 convolution_subtract_fusion
  89.7 0.6 copy-done.1
  90.2 1.0 %multiply_add_fusion = (f32[16,18432]{1,0:T(8,128)S(1)}, f32[16,18432]{1,0:T(8,128)S(1)}) fusion(f32[16,18432]{1,0:T(8,128)S(1)} %convolution_subtract_fusion.2, f32[16,18432]{1,0:T(8,128)S(1)} %copy-done.1, f32[16,18432]{1,0:T(8,128)S(1)} %convolution_subtract_fusion, f32[16,18432]{1,0:T(8,128)S(1)} %fusion.38, bf16[8,18432]{1,0:T(8,128)(2,1)S(1)} %squeeze.58, ...), kind=kOutput, calls=%fused_computation.35 | convolution fusion | flops 30377728 | bytes 7372832 | tf_op jit(solution)/shard_map/dot_general | solution.py:37
  91.3 0.7 fusion.36
  92.0 0.7 fusion.34
  92.8 0.8 fusion.10
  93.6 0.7 fusion.11
  94.4 0.9 pad_maximum_fusion.1
  (32 shorter events, 1.0 us)
Async XLA Ops:
  0.0 46.7 %copy-start = (bf16[1,384,384]{2,1,0:T(8,128)(2,1)S(1)}, bf16[1,384,384]{2,1,0:T(8,128)(2,1)}, u32[]{:S(2)}) copy-start(bf16[1,384,384]{2,1,0:T(8,128)(2,1)} %param.6) | copy-start | bytes 884740
  1.4 19.6 %collective-permute-start.6 = (bf16[4,1,48,384]{3,2,0,1:T(8,128)(2,1)S(1)}, bf16[4,1,48,384]{3,2,0,1:T(8,128)(2,1)S(1)}, u32[]{:S(2)}, u32[]{:S(2)}) collective-permute-start(bf16[4,1,48,384]{3,2,0,1:T(8,128)(2,1)S(1)} %get-tuple-element.15), channel_id=1, source_target_pairs={{0,28},{4,24},{8,20},{12,16},{16,12},{20,8},{24,4},{28,0},{1,29},{... | collective-permute-start | bytes 442376 | tf_op jit(solution)/shard_map/ppermute | solution.py:25
  3.4 17.6 %collective-permute-start.5 = (bf16[4,1,48,384]{3,2,0,1:T(8,128)(2,1)S(1)}, bf16[4,1,48,384]{3,2,0,1:T(8,128)(2,1)S(1)}, u32[]{:S(2)}, u32[]{:S(2)}) collective-permute-start(bf16[4,1,48,384]{3,2,0,1:T(8,128)(2,1)S(1)} %get-tuple-element.16), channel_id=1, source_target_pairs={{0,24},{4,28},{8,16},{12,20},{16,8},{20,12},{24,0},{28,4},{1,25},{... | collective-permute-start | bytes 442376 | tf_op jit(solution)/shard_map/ppermute | solution.py:25
  4.0 16.9 %collective-permute-start.4 = (bf16[4,1,48,384]{3,2,0,1:T(8,128)(2,1)S(1)}, bf16[4,1,48,384]{3,2,0,1:T(8,128)(2,1)S(1)}, u32[]{:S(2)}, u32[]{:S(2)}) collective-permute-start(bf16[4,1,48,384]{3,2,0,1:T(8,128)(2,1)S(1)} %get-tuple-element.17), channel_id=1, source_target_pairs={{0,20},{4,16},{8,28},{12,24},{16,4},{20,0},{24,12},{28,8},{1,21},{... | collective-permute-start | bytes 442376 | tf_op jit(solution)/shard_map/ppermute | solution.py:25
  5.4 15.5 %collective-permute-start.3 = (bf16[4,1,48,384]{3,2,0,1:T(8,128)(2,1)S(1)}, bf16[4,1,48,384]{3,2,0,1:T(8,128)(2,1)S(1)}, u32[]{:S(2)}, u32[]{:S(2)}) collective-permute-start(bf16[4,1,48,384]{3,2,0,1:T(8,128)(2,1)S(1)} %get-tuple-element.18), channel_id=1, source_target_pairs={{0,16},{4,20},{8,24},{12,28},{16,0},{20,4},{24,8},{28,12},{1,17},{... | collective-permute-start | bytes 442376 | tf_op jit(solution)/shard_map/ppermute | solution.py:25
  5.9 1.4 %collective-permute-start = (bf16[4,1,48,384]{3,2,0,1:T(8,128)(2,1)S(1)}, bf16[4,1,48,384]{3,2,0,1:T(8,128)(2,1)S(1)}, u32[]{:S(2)}, u32[]{:S(2)}) collective-permute-start(bf16[4,1,48,384]{3,2,0,1:T(8,128)(2,1)S(1)} %get-tuple-element.21), channel_id=1, source_target_pairs={{0,4},{4,0},{8,12},{12,8},{16,20},{20,16},{24,28},{28,24},{1,5},{5... | collective-permute-start | bytes 442376 | tf_op jit(solution)/shard_map/ppermute | solution.py:25
  7.3 7.7 %collective-permute-start.1 = (bf16[4,1,48,384]{3,2,0,1:T(8,128)(2,1)S(1)}, bf16[4,1,48,384]{3,2,0,1:T(8,128)(2,1)S(1)}, u32[]{:S(2)}, u32[]{:S(2)}) collective-permute-start(bf16[4,1,48,384]{3,2,0,1:T(8,128)(2,1)S(1)} %get-tuple-element.20), channel_id=1, source_target_pairs={{0,8},{4,12},{8,0},{12,4},{16,24},{20,28},{24,16},{28,20},{1,9},{5... | collective-permute-start | bytes 442376 | tf_op jit(solution)/shard_map/ppermute | solution.py:25
  15.0 5.9 %collective-permute-start.2 = (bf16[4,1,48,384]{3,2,0,1:T(8,128)(2,1)S(1)}, bf16[4,1,48,384]{3,2,0,1:T(8,128)(2,1)S(1)}, u32[]{:S(2)}, u32[]{:S(2)}) collective-permute-start(bf16[4,1,48,384]{3,2,0,1:T(8,128)(2,1)S(1)} %get-tuple-element.19), channel_id=1, source_target_pairs={{0,12},{4,8},{8,4},{12,0},{16,28},{20,24},{24,20},{28,16},{1,13},{... | collective-permute-start | bytes 442376 | tf_op jit(solution)/shard_map/ppermute | solution.py:25
  22.0 0.7 copy-start.3
  46.7 6.5 %copy-start.2 = (bf16[1,384,384]{2,1,0:T(8,128)(2,1)S(1)}, bf16[1,384,384]{2,1,0:T(8,128)(2,1)}, u32[]{:S(2)}) copy-start(bf16[1,384,384]{2,1,0:T(8,128)(2,1)} %param.5) | copy-start | bytes 884740
  48.6 15.2 %collective-permute-start.8 = (bf16[2,1,384,384]{3,2,0,1:T(8,128)(2,1)}, bf16[2,1,384,384]{3,2,0,1:T(8,128)(2,1)}, u32[]{:S(2)}, u32[]{:S(2)}) collective-permute-start(bf16[2,1,384,384]{3,2,0,1:T(8,128)(2,1)} %fusion.17), channel_id=1, source_target_pairs={{1,0},{2,1},{3,2},{5,4},{6,5},{7,6},{9,8},{10,9},{11,10},{13,12},{... | collective-permute-start | bytes 1769480 | tf_op jit(solution)/shard_map/ppermute | solution.py:33
  51.8 16.9 %collective-permute-start.7 = (bf16[2,1,384,384]{2,3,0,1:T(8,128)(2,1)}, bf16[2,1,384,384]{2,3,0,1:T(8,128)(2,1)}, u32[]{:S(2)}, u32[]{:S(2)}) collective-permute-start(bf16[2,1,384,384]{2,3,0,1:T(8,128)(2,1)} %copy.41), channel_id=1, source_target_pairs={{0,1},{1,2},{2,3},{4,5},{5,6},{6,7},{8,9},{9,10},{10,11},{12,13},{... | collective-permute-start | bytes 1769480 | tf_op jit(solution)/shard_map/ppermute | solution.py:33
  89.0 1.3 %copy-start.1 = (f32[16,18432]{1,0:T(8,128)S(1)}, f32[16,18432]{1,0:T(8,128)}, u32[]{:S(2)}) copy-start(f32[16,18432]{1,0:T(8,128)} %get-tuple-element.22) | copy-start | bytes 3538948
